TPU v7x, 32 devices: a whole 2x2x4 slice. The times are simulated.
32 devices in a mesh: seq: 16 (over z, y, core), head: 2 (over x).
Axes of the slice: x: 2, y: 2, z: 4, core: 2. Of those that a mesh axis runs over, the one named last changes fastest.
Arguments:
- states: bfloat16 [4096, 4096], P('seq', 'head'), may hold values from -6 to 6
- queries: bfloat16 [4096, 4096], P('seq', 'head'), may hold values from -240 to 240
- w_key: bfloat16 [4096, 1024], P('seq', 'head'), may hold values from -0.09375 to 0.09375
- w_value: bfloat16 [4096, 1024], P('seq', 'head'), may hold values from -0.09375 to 0.09375
- grad_out: bfloat16 [4096, 4096], P('seq', 'head'), may hold values from -6 to 6
- lengths: int32 [16, 4], replicated, may hold values from 16 to 208, as said below
- give_plan: int32 [16], replicated, may hold values from 0 to 128, as said below
Outputs:
- attended: bfloat16 [6144, 4096], P('seq', 'head')
- query_grad: bfloat16 [6144, 4096], P('seq', 'head')
- key_weight_grad: float32 [4096, 1024], P('seq', 'head')
- value_weight_grad: float32 [4096, 1024], P('seq', 'head')
Inputs may be any that keep to these rules, and one draw needn't show every extreme that they name: Each row holds 4 lengths, multiples of 16, summing to 256. give_plan[s] is 0 or 128; where it is 128, shard s's trailing documents fill exactly its last 128 tokens. Some shard gives in every draw.
All inputs are finite; a program needn't handle non-finite values.
Results may differ from a plain program's by a relative error of at most 0.023.
The roundings to bfloat16 on the way count: a program that leaves them out, or rounds other values in their place, can miss the bound.
Values may be sent and summed in bfloat16 or wider, within the bound.
A program may use at most 64 MiB of HBM per device.

v0:
```python
import jax
import jax.numpy as jnp
from jax import lax
from jax.sharding import PartitionSpec as P

HD = 128
GROUP = 4
GIVE = 128
DOCS_DEV = 4


def from_partner(value, axis, apart):
    mask = 2**apart
    pairs = [(source, source ^ mask) for source in range(lax.axis_size(axis))]
    return lax.ppermute(value, axis, pairs)


def segment_ids(row_lengths, row_total):
    doc_ends = jnp.cumsum(row_lengths)
    places = jnp.arange(row_total, dtype=jnp.int32)
    return jnp.sum((places[:, None] >= doc_ends[None, :]).astype(jnp.int32), axis=1)


def attend_block(queries, keys, values, grad_out, segment, usable):
    row_count = queries.shape[0]
    kv_count = keys.shape[1] // HD
    score_scale = HD ** (-0.5)
    query_heads = jnp.moveaxis(queries.reshape(row_count, kv_count, GROUP, HD), 2, 0)
    grad_heads = jnp.moveaxis(grad_out.reshape(row_count, kv_count, GROUP, HD), 2, 0)
    key_heads = keys.reshape(row_count, kv_count, HD)
    value_heads = values.reshape(row_count, kv_count, HD)
    places = jnp.arange(row_count, dtype=jnp.int32)
    allowed = (segment[:, None] == segment[None, :]) & (places[None, :] <= places[:, None])
    allowed = allowed & usable[:, None] & usable[None, :]
    usable_rows = usable[:, None].astype(jnp.float32)

    def one_head(carry, members):
        head_query, head_grad = members
        scores = (
            jnp.einsum("tkd,ukd->ktu", head_query, key_heads, preferred_element_type=jnp.float32)
            * score_scale
        )
        scores = jnp.where(allowed, scores, jnp.float32(-1e30))
        row_max = jnp.max(scores, axis=-1, keepdims=True)
        exponent = jnp.exp(scores - row_max)
        soft_weights = exponent / jnp.sum(exponent, axis=-1, keepdims=True) * usable_rows
        soft_rounded = soft_weights.astype(jnp.bfloat16)
        attended = jnp.einsum(
            "ktu,ukd->tkd", soft_rounded, value_heads, preferred_element_type=jnp.float32
        ).astype(jnp.bfloat16)
        grad_probs = jnp.einsum(
            "tkd,ukd->ktu", head_grad, value_heads, preferred_element_type=jnp.float32
        )
        row_dots = jnp.einsum(
            "tkd,tkd->kt", head_grad.astype(jnp.float32), attended.astype(jnp.float32)
        )
        grad_scores = (soft_weights * (grad_probs - row_dots[..., None])).astype(jnp.bfloat16)
        query_grad = (
            jnp.einsum("ktu,ukd->tkd", grad_scores, key_heads, preferred_element_type=jnp.float32)
            * score_scale
        ).astype(jnp.bfloat16)
        key_total = carry[0] + jnp.einsum(
            "ktu,tkd->ukd", grad_scores, head_query, preferred_element_type=jnp.float32
        )
        value_total = carry[1] + jnp.einsum(
            "ktu,tkd->ukd", soft_rounded, head_grad, preferred_element_type=jnp.float32
        )
        return ((key_total, value_total), (attended, query_grad))

    empty = jnp.zeros((row_count, kv_count, HD), jnp.float32)
    totals, stacked = lax.scan(one_head, (empty, empty), (query_heads, grad_heads))
    attended = jnp.moveaxis(stacked[0], 0, 2)
    query_grad = jnp.moveaxis(stacked[1], 0, 2)
    key_grad = (totals[0] * score_scale).astype(jnp.bfloat16)
    value_grad = totals[1].astype(jnp.bfloat16)
    return (
        attended.reshape(row_count, kv_count * GROUP * HD),
        query_grad.reshape(row_count, kv_count * GROUP * HD),
        key_grad.reshape(row_count, kv_count * HD),
        value_grad.reshape(row_count, kv_count * HD),
    )


def local(states, queries, w_key, w_value, grad_out, lengths, give_plan):
    seq_count = lax.axis_size("seq")
    shard = lax.axis_index("seq")
    partner = jnp.bitwise_xor(shard, seq_count // 2)
    flip_bit = seq_count.bit_length() - 2
    key_rows, value_rows = (
        lax.all_gather(w_key, "seq", axis=0, tiled=True),
        lax.all_gather(w_value, "seq", axis=0, tiled=True),
    )
    width = key_rows.shape[1]
    tok_rows = states.shape[0]
    piece = lax.all_gather(states, "head", axis=1, tiled=True)
    key_sums = jnp.dot(piece, key_rows, preferred_element_type=jnp.float32)
    value_sums = jnp.dot(piece, value_rows, preferred_element_type=jnp.float32)
    keys = key_sums.astype(jnp.bfloat16)
    values = value_sums.astype(jnp.bfloat16)
    own_lengths = lax.dynamic_index_in_dim(lengths, shard, 0, keepdims=False)
    other_lengths = lax.dynamic_index_in_dim(lengths, partner, 0, keepdims=False)
    own_give = lax.dynamic_index_in_dim(give_plan, shard, 0, keepdims=False)
    other_give = lax.dynamic_index_in_dim(give_plan, partner, 0, keepdims=False)
    start_tail = tok_rows - GIVE
    sent = (queries[start_tail:], keys[start_tail:], values[start_tail:], grad_out[start_tail:])
    got_queries, got_keys, got_values, got_grads = from_partner(
        (sent[0], sent[1], sent[2], sent[3]), "seq", flip_bit
    )
    own_segment = segment_ids(own_lengths, tok_rows)
    other_segment = segment_ids(other_lengths, tok_rows)[start_tail:] + DOCS_DEV
    own_usable = jnp.arange(tok_rows, dtype=jnp.int32) < tok_rows - own_give
    other_usable = jnp.arange(GIVE, dtype=jnp.int32) >= GIVE - other_give
    own_parts = attend_block(queries, keys, values, grad_out, own_segment, own_usable)
    other_parts = attend_block(
        got_queries, got_keys, got_values, got_grads, other_segment, other_usable
    )
    attended = jnp.concatenate([own_parts[0], other_parts[0]], axis=0)
    query_grad = jnp.concatenate([own_parts[1], other_parts[1]], axis=0)
    back_keys, back_values = from_partner((other_parts[2], other_parts[3]), "seq", flip_bit)
    pad_rows = ((start_tail, 0), (0, 0))
    key_home = own_parts[2] + jnp.pad(back_keys, pad_rows)
    value_home = own_parts[3] + jnp.pad(back_values, pad_rows)
    grads_home = jnp.concatenate([key_home, value_home], axis=1)
    term_sums = lax.dot_general(
        lax.all_gather(states, "head", axis=1, tiled=True),
        grads_home,
        (((0,), (0,)), ((), ())),
        preferred_element_type=jnp.float32,
    )
    summed = lax.psum_scatter(term_sums, "seq", scatter_dimension=0, tiled=True)
    return (attended, query_grad, summed[:, :width], summed[:, width:])


def solution(mesh):
    return jax.shard_map(
        local,
        mesh=mesh,
        in_specs=(
            P("seq", "head"),
            P("seq", "head"),
            P("seq", "head"),
            P("seq", "head"),
            P("seq", "head"),
            P(),
            P(),
        ),
        out_specs=(P("seq", "head"), P("seq", "head"), P("seq", "head"), P("seq", "head")),
        check_vma=False,
    )
```

profile of v0, /device:TPU:0, one launch (start us, length us, event | category | flops | bytes accessed | tf_op | source)
XLA Modules:
  0.0 443.8 jit_solution(14424001753771788512)
XLA Ops:
  10.9 4.1 collective-permute-start
  14.9 1.3 copy.87
  16.2 1.9 slice.30
  20.9 24.5 %all-gather.4.cloned.1.call-done = bf16[256,4096]{1,0:T(8,128)(2,1)} async-done(((bf16[256,2048]{1,0:T(8,128)(2,1)}), bf16[256,4096]{1,0:T(8,128)(2,1)}) %all-gather.4.cloned.1.call-update) | async-done | bytes 2097168 | tf_op jit(solution)/shard_map/all_gather | solution.py:95
  45.4 54.9 %all-gather.8.cloned.1.call-done = bf16[4096,512]{1,0:T(8,128)(2,1)} async-done(((bf16[256,512]{1,0:T(8,128)(2,1)}), bf16[4096,512]{1,0:T(8,128)(2,1)}) %all-gather.8.cloned.1.call-update) | async-done | bytes 4194320 | tf_op jit(solution)/shard_map/all_gather | solution.py:91
  100.3 4.1 convolution_convert_fusion.2
  105.8 45.6 %all-gather.6.cloned.1.call-done = bf16[4096,512]{1,0:T(8,128)(2,1)} async-done(((bf16[256,512]{1,0:T(8,128)(2,1)}), bf16[4096,512]{1,0:T(8,128)(2,1)}) %all-gather.6.cloned.1.call-update) | async-done | bytes 4194320 | tf_op jit(solution)/shard_map/all_gather | solution.py:90
  151.4 4.1 convolution_convert_fusion.3
  156.2 1.9 collective-permute-start.1
  158.1 1.1 collective-permute-start.3
  159.2 42.3 %while.34 = (s32[]{:T(128)}, f32[256,4,128]{0,2,1:T(8,128)S(1)}, f32[256,4,128]{0,2,1:T(8,128)}, bf16[4,256,4,128]{3,1,2,0:T(8,128)(2,1)}, bf16[4,256,4,128]{3,1...) while((s32[]{:T(128)}, f32[256,4,128]{0,2,1:T(8,128)S(1)}, ...), condition=%wide.region_5.6_spmd.clone, body=%wide.region_2.5_spmd.clone.sunk | while | flops 544147712 | bytes 11564472 | solution.py:71
  160.5 1.4 fusion.197
  161.9 1.8 fusion.198
  163.7 1.6 fusion.199
  165.3 1.5 fusion.201
  167.2 1.0 fusion.202
  170.2 1.4 fusion.197
  171.7 1.8 fusion.198
  173.5 1.6 fusion.199
  175.1 2.5 fusion.201
  178.0 1.0 fusion.202
  181.1 1.4 fusion.197
  182.5 1.8 fusion.198
  184.3 1.6 fusion.199
  185.9 2.5 fusion.201
  188.8 1.1 fusion.202
  191.9 1.4 fusion.197
  193.4 1.8 fusion.198
  195.2 1.6 fusion.199
  196.8 2.5 fusion.201
  199.7 1.1 fusion.202
  203.4 32.1 %while.35 = (s32[]{:T(128)}, f32[128,4,128]{0,2,1:T(8,128)S(1)}, f32[128,4,128]{0,2,1:T(8,128)S(1)}, bf16[4,128,4,128]{3,1,2,0:T(8,128)(2,1)}, bf16[4,128,4,128]...) while((s32[]{:T(128)}, f32[128,4,128]{0,2,1:T(8,128)S(1)}, ...), condition=%wide.region_11.12_spmd.clone, body=%wide.region_8.11_spmd.clone.sunk | while | flops 136397952 | bytes 4799288 | solution.py:71
  204.6 1.2 fusion.220
  205.8 1.4 fusion.221
  207.4 1.3 fusion.224
  208.8 1.1 fusion.223
  212.7 1.2 fusion.220
  213.8 1.4 fusion.221
  215.4 1.3 fusion.224
  216.8 1.1 fusion.223
  220.7 1.2 fusion.220
  221.8 1.4 fusion.221
  223.4 1.3 fusion.224
  224.8 1.1 fusion.223
  228.7 1.2 fusion.220
  229.8 1.4 fusion.221
  231.5 1.3 fusion.224
  232.8 1.1 fusion.223
  235.5 1.9 collective-permute-start.5
  237.5 1.1 collective-permute-start.4
  238.6 9.6 %collective-permute-done.5 = bf16[128,512]{0,1:T(8,128)(2,1)S(1)} collective-permute-done((bf16[128,512]{0,1:T(8,128)(2,1)S(1)}, bf16[128,512]{0,1:T(8,128)(2,1)S(1)}, u32[]{:S(2)}, u32[]{:S(2)}) %collective-permute-start.5) | collective-permute-done | bytes 131104 | tf_op jit(solution)/shard_map/ppermute | solution.py:15
  248.3 1.7 collective-permute-done.4
  250.1 8.1 %convolution_bitcast_fusion.4 = f32[4096,1024]{0,1:T(8,128)} fusion(bf16[256,4096]{1,0:T(8,128)(2,1)S(1)} %copy-done, bf16[256,512]{0,1:T(8,128)(2,1)S(1)} %bitcast_add_fusion, bf16[256,512]{0,1:T(8,128)(2,1)S(1)} %bitcast_add_fusion.1), kind=kOutput, calls=%fused_computation.85 | convolution fusion | flops 2148532224 | bytes 19398656 | tf_op jit(solution)/shard_map/dot_general | solution.py:124
  258.2 1.2 copy-done.3
  261.0 2.1 copy.92
  263.2 1.0 reshape.160
  264.2 1.6 copy.102
  266.1 2.3 copy.100
  268.4 1.5 reshape.167
  270.0 1.9 pad_maximum_fusion
  271.9 162.1 %reduce-scatter.2.cloned.1.call-done = f32[256,1024]{0,1:T(8,128)} async-done(((f32[4096,1024]{0,1:T(8,128)}), f32[256,1024]{0,1:T(8,128)}) %reduce-scatter.2.cloned.1.call-update) | async-done | bytes 1048592 | tf_op jit(solution)/shard_map/reduce_scatter | solution.py:130
  434.0 1.3 fusion.109
  435.3 1.0 copy.104
  436.3 1.0 copy.103
  (111 shorter events, 32.3 us)
Async XLA Ops:
  7.2 2.3 copy-start.1
  7.2 7.8 %copy-start.2 = (bf16[256,2048]{1,0:T(8,128)(2,1)S(1)}, bf16[256,2048]{1,0:T(8,128)(2,1)}, u32[]{:S(2)}) copy-start(bf16[256,2048]{1,0:T(8,128)(2,1)} %param.15) | copy-start | bytes 3145732
  7.2 38.2 %all-gather.4.cloned.1.call-start = ((), (), s32[]{:S(2)}) async-start(), calls=%async_computation.1 | async-start | bytes 3145728 | tf_op jit(solution)/shard_map/all_gather | solution.py:95
  7.9 92.4 %all-gather.8.cloned.1.call-start = ((), (), s32[]{:S(2)}) async-start(), calls=%async_computation.3 | async-start | bytes 4456448 | tf_op jit(solution)/shard_map/all_gather | solution.py:91
  8.7 142.7 %all-gather.6.cloned.1.call-start = ((), (), s32[]{:S(2)}) async-start(), calls=%async_computation.2 | async-start | bytes 4456448 | tf_op jit(solution)/shard_map/all_gather | solution.py:90
  9.4 424.6 %reduce-scatter.2.cloned.1.call-start = ((), (), s32[]{:S(2)}) async-start(), calls=%async_computation.4 | async-start | bytes 17825792 | tf_op jit(solution)/shard_map/reduce_scatter | solution.py:130
  10.0 8.2 %copy-start.5 = (s32[16,4]{0,1:T(4,128)S(1)}, s32[16,4]{0,1:T(4,128)}, u32[]{:S(2)}) copy-start(s32[16,4]{0,1:T(4,128)} %param.16) | copy-start | bytes 772
  10.0 8.8 %copy-start.6 = (s32[16]{0:T(128)S(1)}, s32[16]{0:T(128)}, u32[]{:S(2)}) copy-start(s32[16]{0:T(128)} %param.17) | copy-start | bytes 196
  10.9 192.5 %collective-permute-start = (bf16[128,2048]{0,1:T(8,128)(2,1)}, bf16[128,2048]{0,1:T(8,128)(2,1)}, u32[]{:S(2)}, u32[]{:S(2)}) collective-permute-start(bf16[128,2048]{0,1:T(8,128)(2,1)} %slice.28), channel_id=1, source_target_pairs={{0,16},{2,18},{4,20},{6,22},{8,24},{10,26},{12,28},{14,30},{16,0},... | collective-permute-start | bytes 1572872 | tf_op jit(solution)/shard_map/ppermute | solution.py:15
  18.2 185.2 %collective-permute-start.2 = (bf16[128,2048]{0,1:T(8,128)(2,1)}, bf16[128,2048]{0,1:T(8,128)(2,1)}, u32[]{:S(2)}, u32[]{:S(2)}) collective-permute-start(bf16[128,2048]{0,1:T(8,128)(2,1)} %slice.30), channel_id=1, source_target_pairs={{0,16},{2,18},{4,20},{6,22},{8,24},{10,26},{12,28},{14,30},{16,0},... | collective-permute-start | bytes 1572872 | tf_op jit(solution)/shard_map/ppermute | solution.py:15
  156.2 45.3 %collective-permute-start.1 = (bf16[128,512]{1,0:T(8,128)(2,1)}, bf16[128,512]{1,0:T(8,128)(2,1)}, u32[]{:S(2)}, u32[]{:S(2)}) collective-permute-start(bf16[128,512]{1,0:T(8,128)(2,1)} %slice.29), channel_id=1, source_target_pairs={{0,16},{2,18},{4,20},{6,22},{8,24},{10,26},{12,28},{14,30},{16,0},... | collective-permute-start | bytes 393224 | tf_op jit(solution)/shard_map/ppermute | solution.py:15
  158.1 44.4 %collective-permute-start.3 = (bf16[128,512]{1,0:T(8,128)(2,1)}, bf16[128,512]{1,0:T(8,128)(2,1)}, u32[]{:S(2)}, u32[]{:S(2)}) collective-permute-start(bf16[128,512]{1,0:T(8,128)(2,1)} %slice.31), channel_id=1, source_target_pairs={{0,16},{2,18},{4,20},{6,22},{8,24},{10,26},{12,28},{14,30},{16,0},... | collective-permute-start | bytes 393224 | tf_op jit(solution)/shard_map/ppermute | solution.py:15
  203.4 44.9 %copy-start.4 = (f32[256,4,128]{0,2,1:T(8,128)S(1)}, f32[256,4,128]{0,2,1:T(8,128)}, u32[]{:S(2)}) copy-start(f32[256,4,128]{0,2,1:T(8,128)} %get-tuple-element.130) | copy-start | bytes 1572868
  235.5 14.6 %copy-start = (bf16[256,4096]{1,0:T(8,128)(2,1)S(1)}, bf16[256,4096]{1,0:T(8,128)(2,1)}, u32[]{:S(2)}) copy-start(bf16[256,4096]{1,0:T(8,128)(2,1)} %all-gather.4.cloned.1.call-done) | copy-start | bytes 6291460
  235.5 12.7 %collective-permute-start.5 = (bf16[128,512]{0,1:T(8,128)(2,1)S(1)}, bf16[128,512]{0,1:T(8,128)(2,1)S(1)}, u32[]{:S(2)}, u32[]{:S(2)}) collective-permute-start(bf16[128,512]{0,1:T(8,128)(2,1)S(1)} %bitcast.266), channel_id=1, source_target_pairs={{0,16},{2,18},{4,20},{6,22},{8,24},{10,26},{12,28},{14,30},{16,0},... | collective-permute-start | bytes 393224 | tf_op jit(solution)/shard_map/ppermute | solution.py:15
  237.5 12.5 %collective-permute-start.4 = (bf16[128,512]{0,1:T(8,128)(2,1)S(1)}, bf16[128,512]{0,1:T(8,128)(2,1)S(1)}, u32[]{:S(2)}, u32[]{:S(2)}) collective-permute-start(bf16[128,512]{0,1:T(8,128)(2,1)S(1)} %bitcast.265), channel_id=1, source_target_pairs={{0,16},{2,18},{4,20},{6,22},{8,24},{10,26},{12,28},{14,30},{16,0},... | collective-permute-start | bytes 393224 | tf_op jit(solution)/shard_map/ppermute | solution.py:15
  258.2 1.2 copy-start.3
Sparse Core Ops, SparseCore 0:
  9.5 35.8 all-gather.3
  47.5 52.7 all-gather.7
  102.5 48.8 all-gather.5
  258.3 175.6 reduce-scatter.1
where the time goes:
time: 445 us; the launch traced here: 444 us
  waiting for transfers between devices  301 us (68%)
  matrix products  74.9 us (17%)
  local copies, waits for them, and re-layouts  38.8 us (9%)
  between operations  15.3 us (3%)
  starting transfers between devices  10.3 us (2%)
    reduce_scatter x1, waiting for transfers between devices, local(): summed = lax.psum_scatter(term_sums, 'seq', scatter_dimension=0, tiled=True)  162 us
    all_gather x1, waiting for transfers between devices, local(): lax.all_gather(w_value, 'seq', axis=0, tiled=True)  54.9 us
    all_gather x1, waiting for transfers between devices, local(): lax.all_gather(w_key, 'seq', axis=0, tiled=True)  45.6 us
    all_gather x1, waiting for transfers between devices, local(): piece = lax.all_gather(states, 'head', axis=1, tiled=True)  24.5 us
    dot_general x8, matrix products, one_head(): jnp.einsum('ktu,tkd->ukd', soft_rounded, head_grad, preferred_element_typ...  14.5 us
    dot_general x8, matrix products, one_head(): jnp.einsum('ktu,ukd->tkd', soft_rounded, value_heads, preferred_element_t...  12.9 us
    ppermute x6, waiting for transfers between devices, from_partner(): return lax.ppermute(value, axis, pairs)  11.4 us
    sub x8, matrix products, one_head(): exponent = jnp.exp(scores - row_max)  10.4 us
  transfers between devices with their start and end apart: 10, of which 6 were waited for; matrix products, arithmetic and copies ran while one was open for 16% of the time, Pallas kernels for 0%

commit v1 on v0

v1 whole, which is shorter than its diff:
```python
import functools

import jax
import jax.numpy as jnp
from jax import lax
from jax.experimental import pallas as pl
from jax.experimental.pallas import tpu as pltpu
from jax.sharding import PartitionSpec as P

HD = 128
GROUP = 4
GIVE = 128
QUAD = 4
MESH = pl.DeviceIdType.MESH
F32 = jnp.float32
BF16 = jnp.bfloat16


def greet(peers):
    barrier = pltpu.get_barrier_semaphore()
    for peer in peers:
        pl.semaphore_signal(barrier, inc=1, device_id=peer, device_id_type=MESH)
    pl.semaphore_wait(barrier, len(peers))


def remote(src, dst, send, recv, device):
    return pltpu.make_async_remote_copy(
        src_ref=src, dst_ref=dst, send_sem=send, recv_sem=recv, device_id=device, device_id_type=MESH
    )


def project_kernel(
    chain, heads,
    st_ref, wk_ref, wv_ref,
    keys_ref, values_ref, turned_ref,
    st_all, w_all, acc,
    st_send, st_recv, z_send, z_recv, y_send, y_recv, c_send, c_recv, own_sem, st_own_sem,
):
    seq = lax.axis_index("seq")
    head = lax.axis_index("head")
    z, quad = seq // QUAD, seq % QUAD
    base = z * QUAD
    other_y = base + (quad + 2) % 4
    other_c = base + (quad // 2) * 2 + (quad + 1) % 2
    rows, cols = wk_ref.shape
    wide = QUAD * rows
    pieces = st_ref.shape[1] // wide
    z_peers = [((z + k) % chain) * QUAD + quad for k in range(1, chain)]
    h_peers = [(head + k) % heads for k in range(1, heads)]
    greet(
        [(p, head) for p in z_peers] + [(other_y, head), (other_c, head)] + [(seq, p) for p in h_peers]
    )

    def rows_of(zz, qq):
        return pl.ds(pl.multiple_of((zz * QUAD + qq) * rows, rows), rows)

    def half(ref, at, side):
        return ref.at[at, pl.ds(side * cols, cols)]

    mine = rows_of(z, quad)
    sent = []

    def go(copy):
        copy.start()
        sent.append(copy)

    for side, src in ((0, wk_ref), (1, wv_ref)):
        go(remote(src, half(w_all, mine, side), y_send.at[0, side], y_recv.at[0, side], (other_y, head)))
        for k in range(1, chain):
            go(remote(src, half(w_all, mine, side), z_send.at[k, side], z_recv.at[k, side], (z_peers[k - 1], head)))
        go(remote(src, half(w_all, mine, side), c_send.at[0, 0, side], c_recv.at[0, 0, side], (other_c, head)))
    own = []
    for n in range(pieces):
        part = st_ref.at[:, pl.ds(n * wide, wide)]
        for k in range(1, heads):
            go(remote(part, st_all.at[head * pieces + n], st_send.at[k, n], st_recv.at[k, n], (seq, h_peers[k - 1])))
        own.append(pltpu.make_async_copy(part, st_all.at[head * pieces + n], st_own_sem.at[n]))
    for side, src in ((0, wk_ref), (1, wv_ref)):
        own.append(pltpu.make_async_copy(src, half(w_all, mine, side), own_sem.at[side]))
    for copy in own:
        copy.start()
    for copy in own:
        copy.wait()

    def turn(slot):
        flipped = st_all[slot].T
        for q in range(QUAD):
            turned_ref[q, pl.ds(pl.multiple_of(slot * rows, rows), rows), :] = flipped[q * rows:(q + 1) * rows, :]

    for n in range(pieces):
        turn(head * pieces + n)

    def source(k):
        return (z - k + chain) % chain

    def arrive_z(k):
        for side in range(2):
            block = half(w_all, rows_of(source(k), quad), side)
            remote(block, block, z_send.at[k, side], z_recv.at[k, side], (other_y, head)).wait_recv()
            go(remote(block, block, y_send.at[k, side], y_recv.at[k, side], (other_y, head)))
            go(remote(block, block, c_send.at[k, 0, side], c_recv.at[k, 0, side], (other_c, head)))

    def arrive_y(k):
        for side in range(2):
            block = half(w_all, rows_of(source(k), (quad + 2) % 4), side)
            remote(block, block, y_send.at[k, side], y_recv.at[k, side], (other_y, head)).wait_recv()
            go(remote(block, block, c_send.at[k, 1, side], c_recv.at[k, 1, side], (other_c, head)))

    mate = (quad // 2) * 2 + (quad + 1) % 2

    def arrive_c(k):
        for side in range(2):
            for far, qq in ((0, mate), (1, (mate + 2) % 4)):
                block = half(w_all, rows_of(source(k), qq), side)
                remote(
                    block, block, c_send.at[k, far, side], c_recv.at[k, far, side], (other_c, head)
                ).wait_recv()

    tile = min(2 * cols, 256)

    def multiply(k):
        slot = source(k)
        at = pl.ds(pl.multiple_of(slot * wide, wide), wide)

        def step(t, carry):
            where = pl.ds(pl.multiple_of(t * tile, tile), tile)
            term = jnp.dot(st_all[slot], w_all[at, where], preferred_element_type=F32)
            if k == 0:
                acc[:, where] = term
            else:
                acc[:, where] += term
            return carry

        lax.fori_loop(0, 2 * cols // tile, step, 0)

    for k in range(chain):
        if k:
            arrive_z(k)
        if k == 1:
            for m in range(1, heads):
                for n in range(pieces):
                    slot = ((head - m + heads) % heads) * pieces + n
                    dst = st_all.at[slot]
                    remote(dst, dst, st_send.at[m, n], st_recv.at[m, n], (seq, h_peers[m - 1])).wait_recv()
                    turn(slot)
            arrive_y(0)
        elif k > 1:
            arrive_y(k - 1)
            arrive_c(k - 2)
            multiply(k - 2)
    arrive_y(chain - 1)
    arrive_c(chain - 2)
    multiply(chain - 2)
    arrive_c(chain - 1)
    multiply(chain - 1)
    keys_ref[...] = acc[:, :cols].astype(BF16)
    values_ref[...] = acc[:, cols:].astype(BF16)
    for copy in sent:
        copy.wait_send()


def attend_kernel(
    chain,
    turned_ref, q_ref, go_ref, keys_ref, values_ref, seg_row, seg_col,
    att_ref, dq_ref, got_att, got_dq, dwk_ref, dwv_ref,
    group_states, pair, terms, parts, total, whole,
    s_send, s_recv, p_send, p_recv, t_send, t_recv, h_send, h_recv, own_sem,
):
    seq = lax.axis_index("seq")
    head = lax.axis_index("head")
    z, quad = seq // QUAD, seq % QUAD
    base = z * QUAD
    tok = q_ref.shape[0]
    kv = keys_ref.shape[1] // HD
    rows = dwk_ref.shape[0]
    scale = HD ** (-0.5)
    across = ((z + chain // 2) % chain) * QUAD + quad
    z_peers = [((z + k) % chain) * QUAD + quad for k in range(1, chain)]
    quads = [(quad + i) % QUAD for i in range(QUAD)]
    greet([(p, head) for p in z_peers] + [(base + p, head) for p in quads[1:]])

    def span(i):
        return pl.ds(pl.multiple_of(i * tok, tok), tok)

    def states_copy(i):
        return remote(
            turned_ref.at[quads[i]], group_states.at[:, span(quad)],
            s_send.at[i], s_recv.at[i], (base + quads[i], head),
        )

    for i in range(1, QUAD):
        states_copy(i).start()
    own = pltpu.make_async_copy(turned_ref.at[quad], group_states.at[:, span(quad)], own_sem)
    own.start()
    own.wait()

    def pair_copy(g, i):
        return remote(
            pair.at[g, span(quad), :], pair.at[g, span(quad), :],
            p_send.at[g, i], p_recv.at[g, i], (base + quads[i], head),
        )

    def tail_copy(g, which):
        ref, dst = ((att_ref, got_att), (dq_ref, got_dq))[which]
        at = pl.ds(pl.multiple_of(g * (GROUP * HD), GROUP * HD), GROUP * HD)
        return remote(
            ref.at[pl.ds(tok - GIVE, GIVE), at], dst.at[:, at],
            h_send.at[g, which], h_recv.at[g, which], (across, head),
        )

    def term_copy(g, k):
        to = (z + k) % chain
        return remote(
            terms.at[g, pl.ds(pl.multiple_of(to * rows, rows), rows), :], parts.at[k - 1, g],
            t_send.at[g, k - 1], t_recv.at[g, k - 1], (z_peers[k - 1], head),
        )

    places_r = lax.broadcasted_iota(jnp.int32, (tok, tok), 0)
    places_c = lax.broadcasted_iota(jnp.int32, (tok, tok), 1)
    allowed = (seg_row[...] == seg_col[...]) & (places_c <= places_r)
    nt = (((1,), (1,)), ((), ()))
    tn = (((0,), (0,)), ((), ()))

    def attend(g):
        at = pl.ds(pl.multiple_of(g * HD, HD), HD)
        key, value = keys_ref[:, at], values_ref[:, at]
        dk = dv = None
        for m in range(GROUP):
            col = pl.ds(pl.multiple_of(g * (GROUP * HD) + m * HD, HD), HD)
            query, grad = q_ref[:, col], go_ref[:, col]
            scores = lax.dot_general(query, key, nt, preferred_element_type=F32) * scale
            scores = jnp.where(allowed, scores, F32(-1e30))
            top = jnp.max(scores, axis=-1, keepdims=True)
            grown = jnp.exp(scores - top)
            probs = grown / jnp.sum(grown, axis=-1, keepdims=True)
            low = probs.astype(BF16)
            out = jnp.dot(low, value, preferred_element_type=F32).astype(BF16)
            att_ref[:, col] = out
            grad_probs = lax.dot_general(grad, value, nt, preferred_element_type=F32)
            dots = jnp.sum(grad.astype(F32) * out.astype(F32), axis=-1, keepdims=True)
            slope = (probs * (grad_probs - dots)).astype(BF16)
            dq = jnp.dot(slope, key, preferred_element_type=F32) * scale
            dq_ref[:, col] = dq.astype(BF16)
            dk_m = lax.dot_general(slope, query, tn, preferred_element_type=F32)
            dv_m = lax.dot_general(low, grad, tn, preferred_element_type=F32)
            dk = dk_m if dk is None else dk + dk_m
            dv = dv_m if dv is None else dv + dv_m
        pair[g, span(quad), pl.ds(0, HD)] = (dk * scale).astype(BF16)
        pair[g, span(quad), pl.ds(HD, HD)] = dv.astype(BF16)
        for i in range(1, QUAD):
            pair_copy(g, i).start()
        for which in range(2):
            tail_copy(g, which).start()

    def reduce(g):
        for i in range(1, QUAD):
            pair_copy(g, i).wait_recv()
        whole[...] = jnp.dot(group_states[...], pair[g], preferred_element_type=F32)
        terms[g] = whole[...].astype(BF16)
        for k in range(1, chain):
            term_copy(g, k).start()
        total[g] = whole[pl.ds(pl.multiple_of(z * rows, rows), rows), :]

    def step(g, carry):
        @pl.when(g < kv)
        def _():
            attend(g)

        @pl.when(g == 1)
        def _():
            for i in range(1, QUAD):
                states_copy(i).wait_recv()

        @pl.when(g > 0)
        def _():
            reduce(g - 1)

        return carry

    lax.fori_loop(0, kv + 1, step, 0)
    for g in range(kv):
        value = total[g]
        for k in range(1, chain):
            term_copy(g, k).wait_recv()
            value = value + parts[k - 1, g].astype(F32)
        dwk_ref[:, pl.ds(g * HD, HD)] = value[:, :HD]
        dwv_ref[:, pl.ds(g * HD, HD)] = value[:, HD:]
    for g in range(kv):
        for which in range(2):
            tail_copy(g, which).wait()
        for i in range(1, QUAD):
            pair_copy(g, i).wait_send()
        for k in range(1, chain):
            term_copy(g, k).wait_send()
    for i in range(1, QUAD):
        states_copy(i).wait_send()


def segment_ids(row_lengths, row_total):
    doc_ends = jnp.cumsum(row_lengths)
    places = jnp.arange(row_total, dtype=jnp.int32)
    return jnp.sum((places[:, None] >= doc_ends[None, :]).astype(jnp.int32), axis=1)


def local(states, queries, w_key, w_value, grad_out, lengths, give_plan):
    count, heads = lax.axis_size("seq"), lax.axis_size("head")
    chain = count // QUAD
    shard = lax.axis_index("seq")
    partner = jnp.bitwise_xor(shard, count // 2)
    tok = states.shape[0]
    rows, cols = w_key.shape
    kv = cols // HD
    deep = rows * count
    pieces = states.shape[1] // (QUAD * rows)
    vmem = pl.BlockSpec(memory_space=pltpu.VMEM)
    dma = pltpu.SemaphoreType.DMA
    limit = 56 * 2**20
    keys, values, turned = pl.pallas_call(
        functools.partial(project_kernel, chain, heads),
        out_shape=(
            jax.ShapeDtypeStruct((tok, cols), BF16),
            jax.ShapeDtypeStruct((tok, cols), BF16),
            jax.ShapeDtypeStruct((QUAD, chain * rows, tok), BF16),
        ),
        in_specs=[vmem] * 3,
        out_specs=(vmem,) * 3,
        scratch_shapes=[
            pltpu.VMEM((chain, tok, QUAD * rows), BF16),
            pltpu.VMEM((deep, 2 * cols), BF16),
            pltpu.VMEM((tok, 2 * cols), F32),
            dma((heads, pieces)), dma((heads, pieces)),
            dma((chain, 2)), dma((chain, 2)),
            dma((chain, 2)), dma((chain, 2)),
            dma((chain, 2, 2)), dma((chain, 2, 2)),
            dma((2,)), dma((pieces,)),
        ],
        compiler_params=pltpu.CompilerParams(
            collective_id=0, has_side_effects=True, vmem_limit_bytes=limit
        ),
        name="project",
    )(states, w_key, w_value)
    segment = segment_ids(lax.dynamic_index_in_dim(lengths, shard, 0, keepdims=False), tok)
    att, dq, got_att, got_dq, dwk, dwv = pl.pallas_call(
        functools.partial(attend_kernel, chain),
        out_shape=(
            jax.ShapeDtypeStruct(queries.shape, BF16),
            jax.ShapeDtypeStruct(queries.shape, BF16),
            jax.ShapeDtypeStruct((GIVE, queries.shape[1]), BF16),
            jax.ShapeDtypeStruct((GIVE, queries.shape[1]), BF16),
            jax.ShapeDtypeStruct((rows, cols), F32),
            jax.ShapeDtypeStruct((rows, cols), F32),
        ),
        in_specs=[vmem] * 7,
        out_specs=(vmem,) * 6,
        scratch_shapes=[
            pltpu.VMEM((chain * rows, QUAD * tok), BF16),
            pltpu.VMEM((kv, QUAD * tok, 2 * HD), BF16),
            pltpu.VMEM((kv, chain * rows, 2 * HD), BF16),
            pltpu.VMEM((chain - 1, kv, rows, 2 * HD), BF16),
            pltpu.VMEM((kv, rows, 2 * HD), F32),
            pltpu.VMEM((chain * rows, 2 * HD), F32),
            dma((QUAD,)), dma((QUAD,)),
            dma((kv, QUAD)), dma((kv, QUAD)),
            dma((kv, chain - 1)), dma((kv, chain - 1)),
            dma((kv, 2)), dma((kv, 2)),
            dma,
        ],
        compiler_params=pltpu.CompilerParams(
            collective_id=1, has_side_effects=True, vmem_limit_bytes=limit
        ),
        name="attend",
    )(turned, queries, grad_out, keys, values, segment[:, None], segment[None, :])
    own_give = lax.dynamic_index_in_dim(give_plan, shard, 0, keepdims=False)
    other_give = lax.dynamic_index_in_dim(give_plan, partner, 0, keepdims=False)
    kept = (jnp.arange(tok, dtype=jnp.int32) < tok - own_give)[:, None]
    taken = (jnp.arange(GIVE, dtype=jnp.int32) >= GIVE - other_give)[:, None]

    def place(own, got):
        zero = jnp.zeros((), own.dtype)
        return jnp.concatenate([jnp.where(kept, own, zero), jnp.where(taken, got, zero)], axis=0)

    return (place(att, got_att), place(dq, got_dq), dwk, dwv)


def solution(mesh):
    return jax.shard_map(
        local,
        mesh=mesh,
        in_specs=(
            P("seq", "head"),
            P("seq", "head"),
            P("seq", "head"),
            P("seq", "head"),
            P("seq", "head"),
            P(),
            P(),
        ),
        out_specs=(P("seq", "head"), P("seq", "head"), P("seq", "head"), P("seq", "head")),
        check_vma=False,
    )
```

time: 445 us -> 195 us (0.44)
  waiting for transfers between devices: 301 us -> 0 us
  Pallas kernels: 0 us -> 183 us
  matrix products: 74.9 us -> 0 us
  local copies, waits for them, and re-layouts: 38.8 us -> 4.58 us
  between operations: 15.3 us -> 2.05 us
  starting transfers between devices: 10.3 us -> 0 us
    pallas_call x0 -> x2, Pallas kernels: none -> 183 us  [the longest x1 113 us: local(): pl.pallas_call(functools.partial(attend_kernel, chain), out_shape=(jax.Sh...]
    reduce_scatter x1 -> x0, waiting for transfers between devices: 162 us -> none  [local(): summed = lax.psum_scatter(term_sums, 'seq', scatter_dimension=0, tiled=True)]
    all_gather x3 -> x0, waiting for transfers between devices: 125 us -> none  [the longest x1 54.9 us: local(): lax.all_gather(w_value, 'seq', axis=0, tiled=True)]
    dot_general x43 -> x0, matrix products: 64.5 us -> none  [the longest x8 14.5 us: one_head(): jnp.einsum('ktu,tkd->ukd', soft_rounded, head_grad, preferred_element_typ...]
    ppermute x6 -> x0, waiting for transfers between devices: 11.4 us -> none  [from_partner(): return lax.ppermute(value, axis, pairs)]
    sub x8 -> x0, matrix products: 10.4 us -> none  [one_head(): exponent = jnp.exp(scores - row_max)]
    ppermute x6 -> x0, starting transfers between devices: 10.1 us -> none  [from_partner(): return lax.ppermute(value, axis, pairs)]
    dynamic_slice x17 -> x1, local copies, waits for them, and re-layouts: 9.06 us -> 0.18 us  [local(): lax.dynamic_index_in_dim(lengths, shard, 0, keepdims=False)]
  transfers between devices with their start and end apart: 10 -> 0, of which waited for: 6 -> 0; matrix products, arithmetic and copies ran while one was open for 16% -> 0% of each run, Pallas kernels for 0% -> 0%
where the time goes in v1:
time: 195 us; the launch traced here: 194 us
  Pallas kernels  183 us (94%)
  local copies, waits for them, and re-layouts  4.58 us (2%)
  other arithmetic  4.13 us (2%)
  between operations  2.05 us (1%)
    pallas_call x1, Pallas kernels, local(): pl.pallas_call(functools.partial(attend_kernel, chain), out_shape=(jax.Sh...  113 us
    pallas_call x1, Pallas kernels, local(): pl.pallas_call(functools.partial(project_kernel, chain, heads), out_shape...  69.9 us

profile of v1, /device:TPU:0, one launch (start us, length us, event | category | flops | bytes accessed | tf_op | source)
XLA Modules:
  0.0 194.0 jit_solution(17828105147319947027)
XLA Ops:
  0.6 0.0 copy-start
  0.7 0.7 copy-done
  1.3 0.2 dynamic-slice_reduce_fusion
  1.5 0.2 reduce-window.8
  1.7 1.3 fusion
  4.3 0.1 convert_reduce_fusion
  4.4 0.0 copy-start.5
  4.4 0.8 copy.12.seg_row
  5.2 69.9 %project.1 = (bf16[256,512]{1,0:T(8,128)(2,1)}, bf16[256,512]{1,0:T(8,128)(2,1)}, bf16[4,1024,256]{2,1,0:T(8,128)(2,1)}) custom-call(bf16[256,2048]{1,0:T(8,128)(2,1)} %st_ref.1, bf16[256,512]{1,0:T(8,128)(2,1)} %wk_ref.1, bf16[256,512]{1,0:T(8,128)(2,1)} %wv_ref.1), custom_call_target="tpu_custom_call" | custom-call | tf_op jit(solution)/shard_map/project/pallas_call | solution.py:318
  75.2 0.0 copy-done.5
  75.2 113.3 %attend.1 = (bf16[256,2048]{1,0:T(8,128)(2,1)}, bf16[256,2048]{1,0:T(8,128)(2,1)}, bf16[128,2048]{1,0:T(8,128)(2,1)}, bf16[128,2048]{1,0:T(8,128)(2,1)}, f32[256,512]{1,0:T(8,128)}, /*index=5*/f32[256,512]{1,0:T(8,128)}) custom-call(bf16[4,1024,256]{2,1,0:T(8,128)(2,1)} %get-tuple-element.13.turned_ref, bf16[256,2048]{1,0:T(8,128)(2,1)} %q_ref.1, ...), custom_call_target="tpu_custom_call" | custom-call | tf_op jit(solution)/shard_map/attend/pallas_call | solution.py:343
  188.5 0.0 copy-start.1
  188.5 0.0 copy-start.2
  188.5 1.8 broadcast_select_fusion
  190.4 0.0 copy-done.1
  190.4 0.0 copy-done.2
  190.4 0.1 broadcast_select_fusion.2
  190.5 0.0 copy-start.4
  190.6 0.0 copy-start.3
  190.6 1.9 pad_maximum_fusion
  192.4 0.0 copy-done.4
  192.5 0.8 copy.15
  193.2 0.0 copy-done.3
  193.2 0.8 copy.16
  (2 shorter events, 0.0 us)
Async XLA Ops:
  0.6 0.7 copy-start
  4.4 70.7 %copy-start.5 = (s32[256]{0:T(256)}, s32[256]{0:T(256)S(1)}, u32[]{:S(2)}) copy-start(s32[256]{0:T(256)S(1)} %convert_reduce_fusion) | copy-start | bytes 3076
  188.5 1.9 copy-start.1
  188.5 1.9 copy-start.2
  190.5 1.9 copy-start.4
  190.6 2.7 %copy-start.3 = (f32[256,512]{1,0:T(8,128)S(1)}, f32[256,512]{1,0:T(8,128)}, u32[]{:S(2)}) copy-start(f32[256,512]{1,0:T(8,128)} %get-tuple-element.37) | copy-start | bytes 1572868

commit v2 on v1

--- a/solution.py
+++ b/solution.py
@@ -16,11 +16,26 @@
 BF16 = jnp.bfloat16
 
 
-def greet(peers):
+def greet(peers, along):
+    z, chain, above, below, head = along
     barrier = pltpu.get_barrier_semaphore()
+
+    def call(peer):
+        pl.semaphore_signal(barrier, inc=1, device_id=peer, device_id_type=MESH)
+
     for peer in peers:
-        pl.semaphore_signal(barrier, inc=1, device_id=peer, device_id_type=MESH)
-    pl.semaphore_wait(barrier, len(peers))
+        call(peer)
+
+    @pl.when(z < chain - 1)
+    def _():
+        call((above, head))
+
+    @pl.when(z > 0)
+    def _():
+        call((below, head))
+
+    near = jnp.where(z < chain - 1, 1, 0) + jnp.where(z > 0, 1, 0)
+    pl.semaphore_wait(barrier, len(peers) + near)
 
 
 def remote(src, dst, send, recv, device):
@@ -34,7 +49,7 @@
     st_ref, wk_ref, wv_ref,
     keys_ref, values_ref, turned_ref,
     st_all, w_all, acc,
-    st_send, st_recv, z_send, z_recv, y_send, y_recv, c_send, c_recv, own_sem, st_own_sem,
+    st_send, st_recv, u_send, d_send, z_recv, y_send, y_recv, c_send, c_recv, own_sem, st_own_sem,
 ):
     seq = lax.axis_index("seq")
     head = lax.axis_index("head")
@@ -45,11 +60,9 @@
     rows, cols = wk_ref.shape
     wide = QUAD * rows
     pieces = st_ref.shape[1] // wide
-    z_peers = [((z + k) % chain) * QUAD + quad for k in range(1, chain)]
     h_peers = [(head + k) % heads for k in range(1, heads)]
-    greet(
-        [(p, head) for p in z_peers] + [(other_y, head), (other_c, head)] + [(seq, p) for p in h_peers]
-    )
+    above, below = seq + QUAD, seq - QUAD
+    greet([(other_y, head), (other_c, head)] + [(seq, p) for p in h_peers], along=(z, chain, above, below, head))
 
     def rows_of(zz, qq):
         return pl.ds(pl.multiple_of((zz * QUAD + qq) * rows, rows), rows)
@@ -57,26 +70,63 @@
     def half(ref, at, side):
         return ref.at[at, pl.ds(side * cols, cols)]
 
-    mine = rows_of(z, quad)
+    mate = (quad // 2) * 2 + (quad + 1) % 2
+    sides = ((0, wk_ref), (1, wv_ref))
+
+    def block(zz, qq, side):
+        return half(w_all, rows_of(zz, qq), side)
+
+    def up_copy(zz, side, src=None):
+        at = block(zz, quad, side)
+        return remote(at if src is None else src, at, u_send.at[zz, side], z_recv.at[zz, side], (above, head))
+
+    def down_copy(zz, side, src=None):
+        at = block(zz, quad, side)
+        return remote(at if src is None else src, at, d_send.at[zz, side], z_recv.at[zz, side], (below, head))
+
+    def y_copy(zz, side, src=None):
+        at = block(zz, quad, side)
+        return remote(at if src is None else src, at, y_send.at[zz, side], y_recv.at[zz, side], (other_y, head))
+
+    def c_copy(zz, far, side, src=None):
+        at = block(zz, (quad + 2 * far) % QUAD, side)
+        return remote(
+            at if src is None else src, at, c_send.at[zz, far, side], c_recv.at[zz, far, side], (other_c, head)
+        )
+
+    def y_wait(zz, side):
+        at = block(zz, (quad + 2) % QUAD, side)
+        remote(at, at, y_send.at[zz, side], y_recv.at[zz, side], (other_y, head)).wait_recv()
+
+    def c_wait(zz, far, side):
+        at = block(zz, (mate + 2 * far) % QUAD, side)
+        remote(at, at, c_send.at[zz, far, side], c_recv.at[zz, far, side], (other_c, head)).wait_recv()
+
+    for side, src in sides:
+        y_copy(z, side, src).start()
+
+        @pl.when(z < chain - 1)
+        def _():
+            up_copy(z, side, src).start()
+
+        @pl.when(z > 0)
+        def _():
+            down_copy(z, side, src).start()
+
+        c_copy(z, 0, side, src).start()
+    own = []
     sent = []
-
-    def go(copy):
-        copy.start()
-        sent.append(copy)
-
-    for side, src in ((0, wk_ref), (1, wv_ref)):
-        go(remote(src, half(w_all, mine, side), y_send.at[0, side], y_recv.at[0, side], (other_y, head)))
-        for k in range(1, chain):
-            go(remote(src, half(w_all, mine, side), z_send.at[k, side], z_recv.at[k, side], (z_peers[k - 1], head)))
-        go(remote(src, half(w_all, mine, side), c_send.at[0, 0, side], c_recv.at[0, 0, side], (other_c, head)))
-    own = []
     for n in range(pieces):
         part = st_ref.at[:, pl.ds(n * wide, wide)]
         for k in range(1, heads):
-            go(remote(part, st_all.at[head * pieces + n], st_send.at[k, n], st_recv.at[k, n], (seq, h_peers[k - 1])))
+            copy = remote(
+                part, st_all.at[head * pieces + n], st_send.at[k, n], st_recv.at[k, n], (seq, h_peers[k - 1])
+            )
+            copy.start()
+            sent.append(copy)
         own.append(pltpu.make_async_copy(part, st_all.at[head * pieces + n], st_own_sem.at[n]))
-    for side, src in ((0, wk_ref), (1, wv_ref)):
-        own.append(pltpu.make_async_copy(src, half(w_all, mine, side), own_sem.at[side]))
+    for side, src in sides:
+        own.append(pltpu.make_async_copy(src, block(z, quad, side), own_sem.at[side]))
     for copy in own:
         copy.start()
     for copy in own:
@@ -87,45 +137,40 @@
         for q in range(QUAD):
             turned_ref[q, pl.ds(pl.multiple_of(slot * rows, rows), rows), :] = flipped[q * rows:(q + 1) * rows, :]
 
-    for n in range(pieces):
-        turn(head * pieces + n)
-
-    def source(k):
-        return (z - k + chain) % chain
-
-    def arrive_z(k):
+    def arrive_z(zz, upward):
         for side in range(2):
-            block = half(w_all, rows_of(source(k), quad), side)
-            remote(block, block, z_send.at[k, side], z_recv.at[k, side], (other_y, head)).wait_recv()
-            go(remote(block, block, y_send.at[k, side], y_recv.at[k, side], (other_y, head)))
-            go(remote(block, block, c_send.at[k, 0, side], c_recv.at[k, 0, side], (other_c, head)))
-
-    def arrive_y(k):
+            if upward:
+                up_copy(zz, side).wait_recv()
+
+                @pl.when(z < chain - 1)
+                def _():
+                    up_copy(zz, side).start()
+            else:
+                down_copy(zz, side).wait_recv()
+
+                @pl.when(z > 0)
+                def _():
+                    down_copy(zz, side).start()
+            y_copy(zz, side).start()
+            c_copy(zz, 0, side).start()
+
+    def arrive_y(zz):
         for side in range(2):
-            block = half(w_all, rows_of(source(k), (quad + 2) % 4), side)
-            remote(block, block, y_send.at[k, side], y_recv.at[k, side], (other_y, head)).wait_recv()
-            go(remote(block, block, c_send.at[k, 1, side], c_recv.at[k, 1, side], (other_c, head)))
-
-    mate = (quad // 2) * 2 + (quad + 1) % 2
-
-    def arrive_c(k):
-        for side in range(2):
-            for far, qq in ((0, mate), (1, (mate + 2) % 4)):
-                block = half(w_all, rows_of(source(k), qq), side)
-                remote(
-                    block, block, c_send.at[k, far, side], c_recv.at[k, far, side], (other_c, head)
-                ).wait_recv()
+            y_wait(zz, side)
+            c_copy(zz, 1, side).start()
 
     tile = min(2 * cols, 256)
 
-    def multiply(k):
-        slot = source(k)
-        at = pl.ds(pl.multiple_of(slot * wide, wide), wide)
+    def multiply(zz, first=False):
+        for far in range(2):
+            for side in range(2):
+                c_wait(zz, far, side)
+        at = pl.ds(pl.multiple_of(zz * wide, wide), wide)
 
         def step(t, carry):
             where = pl.ds(pl.multiple_of(t * tile, tile), tile)
-            term = jnp.dot(st_all[slot], w_all[at, where], preferred_element_type=F32)
-            if k == 0:
+            term = jnp.dot(st_all[zz], w_all[at, where], preferred_element_type=F32)
+            if first:
                 acc[:, where] = term
             else:
                 acc[:, where] += term
@@ -133,38 +178,61 @@
 
         lax.fori_loop(0, 2 * cols // tile, step, 0)
 
-    for k in range(chain):
+    def sources(k):
+        if k == 0:
+            return [(z, None, None)]
+        return [(z - k, z >= k, True), (z + k, z + k < chain, False)]
+
+    def each(k, body):
+        if not 0 <= k < chain:
+            return
+        for zz, there, upward in sources(k):
+            if there is None:
+                body(zz, upward)
+            else:
+                pl.when(there)(functools.partial(body, zz, upward))
+
+    for k in range(chain + 2):
         if k:
-            arrive_z(k)
+            each(k, arrive_z)
         if k == 1:
+            for n in range(pieces):
+                turn(head * pieces + n)
+        if k == min(2, chain - 1):
             for m in range(1, heads):
                 for n in range(pieces):
                     slot = ((head - m + heads) % heads) * pieces + n
                     dst = st_all.at[slot]
                     remote(dst, dst, st_send.at[m, n], st_recv.at[m, n], (seq, h_peers[m - 1])).wait_recv()
                     turn(slot)
-            arrive_y(0)
-        elif k > 1:
-            arrive_y(k - 1)
-            arrive_c(k - 2)
-            multiply(k - 2)
-    arrive_y(chain - 1)
-    arrive_c(chain - 2)
-    multiply(chain - 2)
-    arrive_c(chain - 1)
-    multiply(chain - 1)
+        each(k - 1, lambda zz, upward: arrive_y(zz))
+        if k >= 2:
+            each(k - 2, lambda zz, upward: multiply(zz, k == 2))
     keys_ref[...] = acc[:, :cols].astype(BF16)
     values_ref[...] = acc[:, cols:].astype(BF16)
     for copy in sent:
         copy.wait_send()
+    for zz in range(chain):
+        for side in range(2):
+            y_copy(zz, side).wait_send()
+            for far in range(2):
+                c_copy(zz, far, side).wait_send()
+
+            @pl.when((zz <= z) & (z < chain - 1))
+            def _():
+                up_copy(zz, side).wait_send()
+
+            @pl.when((zz >= z) & (z > 0))
+            def _():
+                down_copy(zz, side).wait_send()
 
 
 def attend_kernel(
     chain,
     turned_ref, q_ref, go_ref, keys_ref, values_ref, seg_row, seg_col,
     att_ref, dq_ref, got_att, got_dq, dwk_ref, dwv_ref,
-    group_states, pair, terms, parts, total, whole,
-    s_send, s_recv, p_send, p_recv, t_send, t_recv, h_send, h_recv, own_sem,
+    group_states, pair, terms, sums, ups, downs,
+    s_send, s_recv, p_send, p_recv, u_send, u_recv, d_send, d_recv, h_send, h_recv, own_sem,
 ):
     seq = lax.axis_index("seq")
     head = lax.axis_index("head")
@@ -175,9 +243,11 @@
     rows = dwk_ref.shape[0]
     scale = HD ** (-0.5)
     across = ((z + chain // 2) % chain) * QUAD + quad
-    z_peers = [((z + k) % chain) * QUAD + quad for k in range(1, chain)]
+    above, below = seq + QUAD, seq - QUAD
     quads = [(quad + i) % QUAD for i in range(QUAD)]
-    greet([(p, head) for p in z_peers] + [(base + p, head) for p in quads[1:]])
+    greet(
+        [(across, head)] + [(base + p, head) for p in quads[1:]], along=(z, chain, above, below, head)
+    )
 
     def span(i):
         return pl.ds(pl.multiple_of(i * tok, tok), tok)
@@ -208,11 +278,17 @@
             h_send.at[g, which], h_recv.at[g, which], (across, head),
         )
 
-    def term_copy(g, k):
-        to = (z + k) % chain
+    def rows_of(d):
+        return pl.ds(d * rows, rows)
+
+    def up_copy(g, d):
         return remote(
-            terms.at[g, pl.ds(pl.multiple_of(to * rows, rows), rows), :], parts.at[k - 1, g],
-            t_send.at[g, k - 1], t_recv.at[g, k - 1], (z_peers[k - 1], head),
+            sums.at[g, rows_of(d), :], ups.at[g, rows_of(d), :], u_send.at[g, d], u_recv.at[g, d], (above, head)
+        )
+
+    def down_copy(g, d):
+        return remote(
+            sums.at[g, rows_of(d), :], downs.at[g, rows_of(d), :], d_send.at[g, d], d_recv.at[g, d], (below, head)
         )
 
     places_r = lax.broadcasted_iota(jnp.int32, (tok, tok), 0)
@@ -255,11 +331,46 @@
     def reduce(g):
         for i in range(1, QUAD):
             pair_copy(g, i).wait_recv()
-        whole[...] = jnp.dot(group_states[...], pair[g], preferred_element_type=F32)
-        terms[g] = whole[...].astype(BF16)
-        for k in range(1, chain):
-            term_copy(g, k).start()
-        total[g] = whole[pl.ds(pl.multiple_of(z * rows, rows), rows), :]
+        terms[g] = jnp.dot(group_states[...], pair[g], preferred_element_type=F32)
+        if chain > 1:
+            @pl.when(z == 0)
+            def _():
+                sums[g] = terms[g].astype(BF16)
+                for d in range(chain - 1, 0, -1):
+                    up_copy(g, d).start()
+
+            @pl.when(z == chain - 1)
+            def _():
+                sums[g] = terms[g].astype(BF16)
+                for d in range(chain - 1):
+                    down_copy(g, d).start()
+
+    def pass_on(g):
+        for k in range(chain - 1):
+            for d, there, copy, parts in (
+                (chain - 1 - k, (z > 0) & (z < chain - 1 - k), up_copy, ups),
+                (k, (z < chain - 1) & (z > k), down_copy, downs),
+            ):
+                @pl.when(there)
+                def _():
+                    copy(g, d).wait_recv()
+                    mixed = terms[g, rows_of(d), :] + parts[g, rows_of(d), :].astype(F32)
+                    sums[g, rows_of(d), :] = mixed.astype(BF16)
+                    copy(g, d).start()
+
+    def finish(g):
+        for d in range(chain):
+            @pl.when(z == d)
+            def _():
+                value = terms[g, rows_of(d), :]
+                if d > 0:
+                    up_copy(g, d).wait_recv()
+                    value = value + ups[g, rows_of(d), :].astype(F32)
+                if d < chain - 1:
+                    down_copy(g, d).wait_recv()
+                    value = value + downs[g, rows_of(d), :].astype(F32)
+                dwk_ref[:, pl.ds(g * HD, HD)] = value[:, :HD]
+                dwv_ref[:, pl.ds(g * HD, HD)] = value[:, HD:]
 
     def step(g, carry):
         @pl.when(g < kv)
@@ -279,19 +390,22 @@
 
     lax.fori_loop(0, kv + 1, step, 0)
     for g in range(kv):
-        value = total[g]
-        for k in range(1, chain):
-            term_copy(g, k).wait_recv()
-            value = value + parts[k - 1, g].astype(F32)
-        dwk_ref[:, pl.ds(g * HD, HD)] = value[:, :HD]
-        dwv_ref[:, pl.ds(g * HD, HD)] = value[:, HD:]
+        pass_on(g)
+    for g in range(kv):
+        finish(g)
     for g in range(kv):
         for which in range(2):
             tail_copy(g, which).wait()
         for i in range(1, QUAD):
             pair_copy(g, i).wait_send()
-        for k in range(1, chain):
-            term_copy(g, k).wait_send()
+        for d in range(chain):
+            @pl.when(z < d)
+            def _():
+                up_copy(g, d).wait_send()
+
+            @pl.when(z > d)
+            def _():
+                down_copy(g, d).wait_send()
     for i in range(1, QUAD):
         states_copy(i).wait_send()
 
@@ -329,7 +443,7 @@
             pltpu.VMEM((deep, 2 * cols), BF16),
             pltpu.VMEM((tok, 2 * cols), F32),
             dma((heads, pieces)), dma((heads, pieces)),
-            dma((chain, 2)), dma((chain, 2)),
+            dma((chain, 2)), dma((chain, 2)), dma((chain, 2)),
             dma((chain, 2)), dma((chain, 2)),
             dma((chain, 2, 2)), dma((chain, 2, 2)),
             dma((2,)), dma((pieces,)),
@@ -355,13 +469,14 @@
         scratch_shapes=[
             pltpu.VMEM((chain * rows, QUAD * tok), BF16),
             pltpu.VMEM((kv, QUAD * tok, 2 * HD), BF16),
+            pltpu.VMEM((kv, chain * rows, 2 * HD), F32),
             pltpu.VMEM((kv, chain * rows, 2 * HD), BF16),
-            pltpu.VMEM((chain - 1, kv, rows, 2 * HD), BF16),
-            pltpu.VMEM((kv, rows, 2 * HD), F32),
-            pltpu.VMEM((chain * rows, 2 * HD), F32),
+            pltpu.VMEM((kv, chain * rows, 2 * HD), BF16),
+            pltpu.VMEM((kv, chain * rows, 2 * HD), BF16),
             dma((QUAD,)), dma((QUAD,)),
             dma((kv, QUAD)), dma((kv, QUAD)),
-            dma((kv, chain - 1)), dma((kv, chain - 1)),
+            dma((kv, chain)), dma((kv, chain)),
+            dma((kv, chain)), dma((kv, chain)),
             dma((kv, 2)), dma((kv, 2)),
             dma,
         ],

time: 195 us -> 175 us (0.90)
  Pallas kernels: 183 us -> 164 us
    pallas_call x1, Pallas kernels: 69.9 us -> 56.2 us  [local(): pl.pallas_call(functools.partial(project_kernel, chain, heads), out_shape...]
    pallas_call x1, Pallas kernels: 113 us -> 108 us  [local(): pl.pallas_call(functools.partial(attend_kernel, chain), out_shape=(jax.Sh...]
where the time goes in v2:
time: 175 us
  Pallas kernels  164 us (94%)
  local copies, waits for them, and re-layouts  4.58 us (3%)
  other arithmetic  4.13 us (2%)
  between operations  2.05 us (1%)
    pallas_call x1, Pallas kernels, local(): pl.pallas_call(functools.partial(attend_kernel, chain), out_shape=(jax.Sh...  108 us
    pallas_call x1, Pallas kernels, local(): pl.pallas_call(functools.partial(project_kernel, chain, heads), out_shape...  56.2 us

profile of v2, /device:TPU:0, one launch (start us, length us, event | category | flops | bytes accessed | tf_op | source)
XLA Modules:
  0.0 174.6 jit_solution(13699919396017832890)
XLA Ops:
  0.6 0.0 copy-start
  0.7 0.7 copy-done
  1.3 0.2 dynamic-slice_reduce_fusion
  1.5 0.2 reduce-window.8
  1.7 1.3 fusion
  4.3 0.1 convert_reduce_fusion
  4.4 0.0 copy-start.5
  4.4 0.8 copy.12.seg_row
  5.2 56.2 %project.1 = (bf16[256,512]{1,0:T(8,128)(2,1)}, bf16[256,512]{1,0:T(8,128)(2,1)}, bf16[4,1024,256]{2,1,0:T(8,128)(2,1)}) custom-call(bf16[256,2048]{1,0:T(8,128)(2,1)} %st_ref.1, bf16[256,512]{1,0:T(8,128)(2,1)} %wk_ref.1, bf16[256,512]{1,0:T(8,128)(2,1)} %wv_ref.1), custom_call_target="tpu_custom_call" | custom-call | tf_op jit(solution)/shard_map/project/pallas_call | solution.py:432
  61.4 0.0 copy-done.5
  61.4 107.7 %attend.1 = (bf16[256,2048]{1,0:T(8,128)(2,1)}, bf16[256,2048]{1,0:T(8,128)(2,1)}, bf16[128,2048]{1,0:T(8,128)(2,1)}, bf16[128,2048]{1,0:T(8,128)(2,1)}, f32[256,512]{1,0:T(8,128)}, /*index=5*/f32[256,512]{1,0:T(8,128)}) custom-call(bf16[4,1024,256]{2,1,0:T(8,128)(2,1)} %get-tuple-element.13.turned_ref, bf16[256,2048]{1,0:T(8,128)(2,1)} %q_ref.1, ...), custom_call_target="tpu_custom_call" | custom-call | tf_op jit(solution)/shard_map/attend/pallas_call | solution.py:457
  169.1 0.0 copy-start.1
  169.1 0.0 copy-start.2
  169.1 1.8 %broadcast_select_fusion = (bf16[256,2048]{1,0:T(8,128)(2,1)S(1)}, bf16[256,2048]{1,0:T(8,128)(2,1)S(1)}) fusion(bf16[256,2048]{1,0:T(8,128)(2,1)} %get-tuple-element.18, pred[256]{0:T(512)(128)(4,1)S(1)} %iota_compare_fusion.1, bf16[256,2048]{1,0:T(8,128)(2,1)} %get-tuple-element.16), kind=kLoop, calls=%fused_computation.2 | loop fusion | flops 1048576 | bytes 4194560 | tf_op jit(solution)/shard_map/jit(_where)/select_n | solution.py:495
  170.9 0.0 copy-done.1
  171.0 0.0 copy-done.2
  171.0 0.1 broadcast_select_fusion.2
  171.1 0.0 copy-start.4
  171.1 0.0 copy-start.3
  171.1 1.9 %pad_maximum_fusion = (bf16[384,2048]{1,0:T(8,128)(2,1)}, bf16[384,2048]{1,0:T(8,128)(2,1)}) fusion(bf16[128,2048]{1,0:T(8,128)(2,1)S(1)} %get-tuple-element.25, bf16[256,2048]{1,0:T(8,128)(2,1)S(1)} %get-tuple-element.23, bf16[128,2048]{1,0:T(8,128)(2,1)S(1)} %get-tuple-element.24, bf16[256,2048]{1,0:T(8,128)(2,1)S(1)} %get-tuple-element.22), kind=kLoop, calls=%fused_computation | loop fusion | flops 6291456 | bytes 6291456 | tf_op jit(solution)/shard_map/concatenate | solution.py:495
  173.0 0.0 copy-done.4
  173.0 0.8 copy.15
  173.8 0.0 copy-done.3
  173.8 0.8 copy.16
  (2 shorter events, 0.0 us)
Async XLA Ops:
  0.6 0.7 copy-start
  4.4 57.0 %copy-start.5 = (s32[256]{0:T(256)}, s32[256]{0:T(256)S(1)}, u32[]{:S(2)}) copy-start(s32[256]{0:T(256)S(1)} %convert_reduce_fusion) | copy-start | bytes 3076
  169.1 1.9 %copy-start.1 = (bf16[128,2048]{1,0:T(8,128)(2,1)S(1)}, bf16[128,2048]{1,0:T(8,128)(2,1)}, u32[]{:S(2)}) copy-start(bf16[128,2048]{1,0:T(8,128)(2,1)} %get-tuple-element.17) | copy-start | bytes 1572868
  169.1 1.9 %copy-start.2 = (bf16[128,2048]{1,0:T(8,128)(2,1)S(1)}, bf16[128,2048]{1,0:T(8,128)(2,1)}, u32[]{:S(2)}) copy-start(bf16[128,2048]{1,0:T(8,128)(2,1)} %get-tuple-element.19) | copy-start | bytes 1572868
  171.1 1.9 %copy-start.4 = (f32[256,512]{1,0:T(8,128)S(1)}, f32[256,512]{1,0:T(8,128)}, u32[]{:S(2)}) copy-start(f32[256,512]{1,0:T(8,128)} %get-tuple-element.36) | copy-start | bytes 1572868
  171.1 2.7 %copy-start.3 = (f32[256,512]{1,0:T(8,128)S(1)}, f32[256,512]{1,0:T(8,128)}, u32[]{:S(2)}) copy-start(f32[256,512]{1,0:T(8,128)} %get-tuple-element.37) | copy-start | bytes 1572868

commit v3 on v2

--- a/solution.py
+++ b/solution.py
@@ -270,12 +270,12 @@
             p_send.at[g, i], p_recv.at[g, i], (base + quads[i], head),
         )
 
-    def tail_copy(g, which):
+    def tail_copy(g, m, which):
         ref, dst = ((att_ref, got_att), (dq_ref, got_dq))[which]
-        at = pl.ds(pl.multiple_of(g * (GROUP * HD), GROUP * HD), GROUP * HD)
+        at = pl.ds(pl.multiple_of(g * (GROUP * HD) + m * HD, HD), HD)
         return remote(
             ref.at[pl.ds(tok - GIVE, GIVE), at], dst.at[:, at],
-            h_send.at[g, which], h_recv.at[g, which], (across, head),
+            h_send.at[g, m, which], h_recv.at[g, m, which], (across, head),
         )
 
     def rows_of(d):
@@ -317,6 +317,8 @@
             slope = (probs * (grad_probs - dots)).astype(BF16)
             dq = jnp.dot(slope, key, preferred_element_type=F32) * scale
             dq_ref[:, col] = dq.astype(BF16)
+            for which in range(2):
+                tail_copy(g, m, which).start()
             dk_m = lax.dot_general(slope, query, tn, preferred_element_type=F32)
             dv_m = lax.dot_general(low, grad, tn, preferred_element_type=F32)
             dk = dk_m if dk is None else dk + dk_m
@@ -325,8 +327,6 @@
         pair[g, span(quad), pl.ds(HD, HD)] = dv.astype(BF16)
         for i in range(1, QUAD):
             pair_copy(g, i).start()
-        for which in range(2):
-            tail_copy(g, which).start()
 
     def reduce(g):
         for i in range(1, QUAD):
@@ -345,18 +345,27 @@
                 for d in range(chain - 1):
                     down_copy(g, d).start()
 
-    def pass_on(g):
-        for k in range(chain - 1):
-            for d, there, copy, parts in (
-                (chain - 1 - k, (z > 0) & (z < chain - 1 - k), up_copy, ups),
-                (k, (z < chain - 1) & (z > k), down_copy, downs),
-            ):
-                @pl.when(there)
-                def _():
-                    copy(g, d).wait_recv()
-                    mixed = terms[g, rows_of(d), :] + parts[g, rows_of(d), :].astype(F32)
-                    sums[g, rows_of(d), :] = mixed.astype(BF16)
-                    copy(g, d).start()
+    def pass_one(g, d, there, copy, parts):
+        @pl.when(there)
+        def _():
+            copy(g, d).wait_recv()
+            mixed = terms[g, rows_of(d), :] + parts[g, rows_of(d), :].astype(F32)
+            sums[g, rows_of(d), :] = mixed.astype(BF16)
+            copy(g, d).start()
+
+    def pass_up(g):
+        for d in range(chain - 1, 1, -1):
+            pass_one(g, d, (z > 0) & (z < d), up_copy, ups)
+
+    def pass_down(g):
+        for d in range(chain - 2):
+            pass_one(g, d, (z < chain - 1) & (z > d), down_copy, downs)
+
+    low_side = z < chain // 2
+
+    def pass_on(g, early):
+        pl.when(low_side)(lambda: pass_up(g) if early else pass_down(g))
+        pl.when(jnp.logical_not(low_side))(lambda: pass_down(g) if early else pass_up(g))
 
     def finish(g):
         for d in range(chain):
@@ -382,20 +391,27 @@
             for i in range(1, QUAD):
                 states_copy(i).wait_recv()
 
-        @pl.when(g > 0)
+        @pl.when((g > 0) & (g < kv + 1))
         def _():
             reduce(g - 1)
 
+        @pl.when((g > 1) & (g < kv + 2))
+        def _():
+            pass_on(g - 2, True)
+
+        @pl.when(g > 2)
+        def _():
+            pass_on(g - 3, False)
+
         return carry
 
-    lax.fori_loop(0, kv + 1, step, 0)
-    for g in range(kv):
-        pass_on(g)
+    lax.fori_loop(0, kv + 3, step, 0)
     for g in range(kv):
         finish(g)
     for g in range(kv):
-        for which in range(2):
-            tail_copy(g, which).wait()
+        for m in range(GROUP):
+            for which in range(2):
+                tail_copy(g, m, which).wait()
         for i in range(1, QUAD):
             pair_copy(g, i).wait_send()
         for d in range(chain):
@@ -477,7 +493,7 @@
             dma((kv, QUAD)), dma((kv, QUAD)),
             dma((kv, chain)), dma((kv, chain)),
             dma((kv, chain)), dma((kv, chain)),
-            dma((kv, 2)), dma((kv, 2)),
+            dma((kv, GROUP, 2)), dma((kv, GROUP, 2)),
             dma,
         ],
         compiler_params=pltpu.CompilerParams(

time: 175 us -> 156 us (0.89); the launches traced: 175 us -> 153 us
  Pallas kernels: 164 us -> 142 us
    pallas_call x1, Pallas kernels: 108 us -> 86.3 us  [local(): pl.pallas_call(functools.partial(attend_kernel, chain), out_shape=(jax.Sh...]
where the time goes in v3:
time: 156 us; the launch traced here: 153 us
  Pallas kernels  142 us (91%)
  local copies, waits for them, and re-layouts  4.58 us (3%)
  other arithmetic  4.13 us (3%)
  between operations  2.05 us (1%)
    pallas_call x1, Pallas kernels, local(): pl.pallas_call(functools.partial(attend_kernel, chain), out_shape=(jax.Sh...  86.3 us
    pallas_call x1, Pallas kernels, local(): pl.pallas_call(functools.partial(project_kernel, chain, heads), out_shape...  56.2 us

profile of v3, /device:TPU:0, one launch (start us, length us, event | category | flops | bytes accessed | tf_op | source)
XLA Modules:
  0.0 153.2 jit_solution(4997777652940658575)
XLA Ops:
  0.6 0.0 copy-start
  0.7 0.7 copy-done
  1.3 0.2 dynamic-slice_reduce_fusion
  1.5 0.2 reduce-window.8
  1.7 1.3 fusion
  4.3 0.1 convert_reduce_fusion
  4.4 0.0 copy-start.5
  4.4 0.8 copy.12.seg_row
  5.2 56.2 %project.1 = (bf16[256,512]{1,0:T(8,128)(2,1)}, bf16[256,512]{1,0:T(8,128)(2,1)}, bf16[4,1024,256]{2,1,0:T(8,128)(2,1)}) custom-call(bf16[256,2048]{1,0:T(8,128)(2,1)} %st_ref.1, bf16[256,512]{1,0:T(8,128)(2,1)} %wk_ref.1, bf16[256,512]{1,0:T(8,128)(2,1)} %wv_ref.1), custom_call_target="tpu_custom_call" | custom-call | tf_op jit(solution)/shard_map/project/pallas_call | solution.py:448
  61.4 0.0 copy-done.5
  61.4 86.3 %attend.1 = (bf16[256,2048]{1,0:T(8,128)(2,1)}, bf16[256,2048]{1,0:T(8,128)(2,1)}, bf16[128,2048]{1,0:T(8,128)(2,1)}, bf16[128,2048]{1,0:T(8,128)(2,1)}, f32[256,512]{1,0:T(8,128)}, /*index=5*/f32[256,512]{1,0:T(8,128)}) custom-call(bf16[4,1024,256]{2,1,0:T(8,128)(2,1)} %get-tuple-element.13.turned_ref, bf16[256,2048]{1,0:T(8,128)(2,1)} %q_ref.1, ...), custom_call_target="tpu_custom_call" | custom-call | tf_op jit(solution)/shard_map/attend/pallas_call | solution.py:473
  147.7 0.0 copy-start.1
  147.7 0.0 copy-start.2
  147.8 1.8 %broadcast_select_fusion = (bf16[256,2048]{1,0:T(8,128)(2,1)S(1)}, bf16[256,2048]{1,0:T(8,128)(2,1)S(1)}) fusion(bf16[256,2048]{1,0:T(8,128)(2,1)} %get-tuple-element.18, pred[256]{0:T(512)(128)(4,1)S(1)} %iota_compare_fusion.1, bf16[256,2048]{1,0:T(8,128)(2,1)} %get-tuple-element.16), kind=kLoop, calls=%fused_computation.2 | loop fusion | flops 1048576 | bytes 4194560 | tf_op jit(solution)/shard_map/jit(_where)/select_n | solution.py:511
  149.6 0.0 copy-done.1
  149.6 0.0 copy-done.2
  149.6 0.1 broadcast_select_fusion.2
  149.8 0.0 copy-start.4
  149.8 0.0 copy-start.3
  149.8 1.9 %pad_maximum_fusion = (bf16[384,2048]{1,0:T(8,128)(2,1)}, bf16[384,2048]{1,0:T(8,128)(2,1)}) fusion(bf16[128,2048]{1,0:T(8,128)(2,1)S(1)} %get-tuple-element.25, bf16[256,2048]{1,0:T(8,128)(2,1)S(1)} %get-tuple-element.23, bf16[128,2048]{1,0:T(8,128)(2,1)S(1)} %get-tuple-element.24, bf16[256,2048]{1,0:T(8,128)(2,1)S(1)} %get-tuple-element.22), kind=kLoop, calls=%fused_computation | loop fusion | flops 6291456 | bytes 6291456 | tf_op jit(solution)/shard_map/concatenate | solution.py:511
  151.7 0.0 copy-done.4
  151.7 0.8 copy.15
  152.5 0.0 copy-done.3
  152.5 0.8 copy.16
  (2 shorter events, 0.0 us)
Async XLA Ops:
  0.6 0.7 copy-start
  4.4 57.0 %copy-start.5 = (s32[256]{0:T(256)}, s32[256]{0:T(256)S(1)}, u32[]{:S(2)}) copy-start(s32[256]{0:T(256)S(1)} %convert_reduce_fusion) | copy-start | bytes 3076
  147.7 1.9 %copy-start.1 = (bf16[128,2048]{1,0:T(8,128)(2,1)S(1)}, bf16[128,2048]{1,0:T(8,128)(2,1)}, u32[]{:S(2)}) copy-start(bf16[128,2048]{1,0:T(8,128)(2,1)} %get-tuple-element.17) | copy-start | bytes 1572868
  147.7 1.9 %copy-start.2 = (bf16[128,2048]{1,0:T(8,128)(2,1)S(1)}, bf16[128,2048]{1,0:T(8,128)(2,1)}, u32[]{:S(2)}) copy-start(bf16[128,2048]{1,0:T(8,128)(2,1)} %get-tuple-element.19) | copy-start | bytes 1572868
  149.8 1.9 %copy-start.4 = (f32[256,512]{1,0:T(8,128)S(1)}, f32[256,512]{1,0:T(8,128)}, u32[]{:S(2)}) copy-start(f32[256,512]{1,0:T(8,128)} %get-tuple-element.36) | copy-start | bytes 1572868
  149.8 2.7 %copy-start.3 = (f32[256,512]{1,0:T(8,128)S(1)}, f32[256,512]{1,0:T(8,128)}, u32[]{:S(2)}) copy-start(f32[256,512]{1,0:T(8,128)} %get-tuple-element.37) | copy-start | bytes 1572868

commit v4 on v3

--- a/solution.py
+++ b/solution.py
@@ -228,11 +228,11 @@
 
 
 def attend_kernel(
-    chain,
+    chain, heads,
     turned_ref, q_ref, go_ref, keys_ref, values_ref, seg_row, seg_col,
     att_ref, dq_ref, got_att, got_dq, dwk_ref, dwv_ref,
     group_states, pair, terms, sums, ups, downs,
-    s_send, s_recv, p_send, p_recv, u_send, u_recv, d_send, d_recv, h_send, h_recv, own_sem,
+    s_send, s_recv, x_send, x_recv, p_send, p_recv, u_send, u_recv, d_send, d_recv, h_send, h_recv, own_sem,
 ):
     seq = lax.axis_index("seq")
     head = lax.axis_index("head")
@@ -245,18 +245,29 @@
     across = ((z + chain // 2) % chain) * QUAD + quad
     above, below = seq + QUAD, seq - QUAD
     quads = [(quad + i) % QUAD for i in range(QUAD)]
+    mate = (quad // 2) * 2 + (quad + 1) % 2
+    h_peers = [(head + k) % heads for k in range(1, heads)]
+    part = (chain // heads) * rows
     greet(
-        [(across, head)] + [(base + p, head) for p in quads[1:]], along=(z, chain, above, below, head)
+        [(across, head)] + [(base + p, head) for p in quads[1:]] + [(seq, p) for p in h_peers],
+        along=(z, chain, above, below, head)
     )
 
     def span(i):
         return pl.ds(pl.multiple_of(i * tok, tok), tok)
 
+    def share(hh):
+        return pl.ds(pl.multiple_of(hh * part, part), part)
+
     def states_copy(i):
         return remote(
-            turned_ref.at[quads[i]], group_states.at[:, span(quad)],
+            turned_ref.at[quads[i], share(head), :], group_states.at[share(head), span(quad)],
             s_send.at[i], s_recv.at[i], (base + quads[i], head),
         )
+
+    def share_copy(i, k, hh):
+        at = group_states.at[share(hh), span((quad - i + QUAD) % QUAD)]
+        return remote(at, at, x_send.at[i, k], x_recv.at[i, k], (seq, h_peers[k - 1]))
 
     for i in range(1, QUAD):
         states_copy(i).start()
@@ -265,10 +276,9 @@
     own.wait()
 
     def pair_copy(g, i):
-        return remote(
-            pair.at[g, span(quad), :], pair.at[g, span(quad), :],
-            p_send.at[g, i], p_recv.at[g, i], (base + quads[i], head),
-        )
+        at = pair.at[g, span((quad + 2) % QUAD if i == 3 else quad), :]
+        to = (quad + 2) % QUAD if i == 2 else mate
+        return remote(at, at, p_send.at[g, i], p_recv.at[g, i], (base + to, head))
 
     def tail_copy(g, m, which):
         ref, dst = ((att_ref, got_att), (dq_ref, got_dq))[which]
@@ -325,12 +335,12 @@
             dv = dv_m if dv is None else dv + dv_m
         pair[g, span(quad), pl.ds(0, HD)] = (dk * scale).astype(BF16)
         pair[g, span(quad), pl.ds(HD, HD)] = dv.astype(BF16)
-        for i in range(1, QUAD):
-            pair_copy(g, i).start()
+        pair_copy(g, 2).start()
+        pair_copy(g, 1).start()
 
     def reduce(g):
-        for i in range(1, QUAD):
-            pair_copy(g, i).wait_recv()
+        pair_copy(g, 1).wait_recv()
+        pair_copy(g, 3).wait_recv()
         terms[g] = jnp.dot(group_states[...], pair[g], preferred_element_type=F32)
         if chain > 1:
             @pl.when(z == 0)
@@ -390,22 +400,35 @@
         def _():
             for i in range(1, QUAD):
                 states_copy(i).wait_recv()
+                for k in range(1, heads):
+                    share_copy(i, k, head).start()
 
         @pl.when((g > 0) & (g < kv + 1))
         def _():
-            reduce(g - 1)
+            pair_copy(g - 1, 2).wait_recv()
+            pair_copy(g - 1, 3).start()
+
+        @pl.when(g == 2)
+        def _():
+            for i in range(1, QUAD):
+                for k in range(1, heads):
+                    share_copy(i, k, (head - k + heads) % heads).wait_recv()
 
         @pl.when((g > 1) & (g < kv + 2))
         def _():
-            pass_on(g - 2, True)
-
-        @pl.when(g > 2)
-        def _():
-            pass_on(g - 3, False)
+            reduce(g - 2)
+
+        @pl.when((g > 2) & (g < kv + 3))
+        def _():
+            pass_on(g - 3, True)
+
+        @pl.when(g > 3)
+        def _():
+            pass_on(g - 4, False)
 
         return carry
 
-    lax.fori_loop(0, kv + 3, step, 0)
+    lax.fori_loop(0, kv + 4, step, 0)
     for g in range(kv):
         finish(g)
     for g in range(kv):
@@ -424,6 +447,8 @@
                 down_copy(g, d).wait_send()
     for i in range(1, QUAD):
         states_copy(i).wait_send()
+        for k in range(1, heads):
+            share_copy(i, k, head).wait_send()
 
 
 def segment_ids(row_lengths, row_total):
@@ -471,7 +496,7 @@
     )(states, w_key, w_value)
     segment = segment_ids(lax.dynamic_index_in_dim(lengths, shard, 0, keepdims=False), tok)
     att, dq, got_att, got_dq, dwk, dwv = pl.pallas_call(
-        functools.partial(attend_kernel, chain),
+        functools.partial(attend_kernel, chain, heads),
         out_shape=(
             jax.ShapeDtypeStruct(queries.shape, BF16),
             jax.ShapeDtypeStruct(queries.shape, BF16),
@@ -490,6 +515,7 @@
             pltpu.VMEM((kv, chain * rows, 2 * HD), BF16),
             pltpu.VMEM((kv, chain * rows, 2 * HD), BF16),
             dma((QUAD,)), dma((QUAD,)),
+            dma((QUAD, heads)), dma((QUAD, heads)),
             dma((kv, QUAD)), dma((kv, QUAD)),
             dma((kv, chain)), dma((kv, chain)),
             dma((kv, chain)), dma((kv, chain)),

time: 156 us -> 148 us (0.949); the launches traced: 153 us -> 148 us
  Pallas kernels: 142 us -> 137 us
    pallas_call x1, Pallas kernels: 86.3 us -> 81.2 us  [local(): pl.pallas_call(functools.partial(attend_kernel, chain, heads), out_shape=...]
where the time goes in v4:
time: 148 us
  Pallas kernels  137 us (93%)
  local copies, waits for them, and re-layouts  4.58 us (3%)
  other arithmetic  4.13 us (3%)
  between operations  2.05 us (1%)
    pallas_call x1, Pallas kernels, local(): pl.pallas_call(functools.partial(attend_kernel, chain, heads), out_shape=...  81.2 us
    pallas_call x1, Pallas kernels, local(): pl.pallas_call(functools.partial(project_kernel, chain, heads), out_shape...  56.2 us

profile of v4, /device:TPU:0, one launch (start us, length us, event | category | flops | bytes accessed | tf_op | source)
XLA Modules:
  0.0 148.2 jit_solution(9056134866761940829)
XLA Ops:
  0.6 0.0 copy-start
  0.7 0.7 copy-done
  1.3 0.2 dynamic-slice_reduce_fusion
  1.5 0.2 reduce-window.8
  1.7 1.3 fusion
  4.3 0.1 convert_reduce_fusion
  4.4 0.0 copy-start.5
  4.4 0.8 copy.12.seg_row
  5.2 56.2 %project.1 = (bf16[256,512]{1,0:T(8,128)(2,1)}, bf16[256,512]{1,0:T(8,128)(2,1)}, bf16[4,1024,256]{2,1,0:T(8,128)(2,1)}) custom-call(bf16[256,2048]{1,0:T(8,128)(2,1)} %st_ref.1, bf16[256,512]{1,0:T(8,128)(2,1)} %wk_ref.1, bf16[256,512]{1,0:T(8,128)(2,1)} %wv_ref.1), custom_call_target="tpu_custom_call" | custom-call | tf_op jit(solution)/shard_map/project/pallas_call | solution.py:473
  61.4 0.0 copy-done.5
  61.4 81.2 %attend.1 = (bf16[256,2048]{1,0:T(8,128)(2,1)}, bf16[256,2048]{1,0:T(8,128)(2,1)}, bf16[128,2048]{1,0:T(8,128)(2,1)}, bf16[128,2048]{1,0:T(8,128)(2,1)}, f32[256,512]{1,0:T(8,128)}, /*index=5*/f32[256,512]{1,0:T(8,128)}) custom-call(bf16[4,1024,256]{2,1,0:T(8,128)(2,1)} %get-tuple-element.13.turned_ref, bf16[256,2048]{1,0:T(8,128)(2,1)} %q_ref.1, ...), custom_call_target="tpu_custom_call" | custom-call | tf_op jit(solution)/shard_map/attend/pallas_call | solution.py:498
  142.6 0.0 copy-start.1
  142.6 0.0 copy-start.2
  142.7 1.8 %broadcast_select_fusion = (bf16[256,2048]{1,0:T(8,128)(2,1)S(1)}, bf16[256,2048]{1,0:T(8,128)(2,1)S(1)}) fusion(bf16[256,2048]{1,0:T(8,128)(2,1)} %get-tuple-element.18, pred[256]{0:T(512)(128)(4,1)S(1)} %iota_compare_fusion.1, bf16[256,2048]{1,0:T(8,128)(2,1)} %get-tuple-element.16), kind=kLoop, calls=%fused_computation.2 | loop fusion | flops 1048576 | bytes 4194560 | tf_op jit(solution)/shard_map/jit(_where)/select_n | solution.py:537
  144.5 0.0 copy-done.1
  144.5 0.0 copy-done.2
  144.5 0.1 broadcast_select_fusion.2
  144.7 0.0 copy-start.4
  144.7 0.0 copy-start.3
  144.7 1.9 %pad_maximum_fusion = (bf16[384,2048]{1,0:T(8,128)(2,1)}, bf16[384,2048]{1,0:T(8,128)(2,1)}) fusion(bf16[128,2048]{1,0:T(8,128)(2,1)S(1)} %get-tuple-element.25, bf16[256,2048]{1,0:T(8,128)(2,1)S(1)} %get-tuple-element.23, bf16[128,2048]{1,0:T(8,128)(2,1)S(1)} %get-tuple-element.24, bf16[256,2048]{1,0:T(8,128)(2,1)S(1)} %get-tuple-element.22), kind=kLoop, calls=%fused_computation | loop fusion | flops 6291456 | bytes 6291456 | tf_op jit(solution)/shard_map/concatenate | solution.py:537
  146.6 0.0 copy-done.4
  146.6 0.8 copy.15
  147.4 0.0 copy-done.3
  147.4 0.8 copy.16
  (2 shorter events, 0.0 us)
Async XLA Ops:
  0.6 0.7 copy-start
  4.4 57.0 %copy-start.5 = (s32[256]{0:T(256)}, s32[256]{0:T(256)S(1)}, u32[]{:S(2)}) copy-start(s32[256]{0:T(256)S(1)} %convert_reduce_fusion) | copy-start | bytes 3076
  142.6 1.9 %copy-start.1 = (bf16[128,2048]{1,0:T(8,128)(2,1)S(1)}, bf16[128,2048]{1,0:T(8,128)(2,1)}, u32[]{:S(2)}) copy-start(bf16[128,2048]{1,0:T(8,128)(2,1)} %get-tuple-element.17) | copy-start | bytes 1572868
  142.6 1.9 %copy-start.2 = (bf16[128,2048]{1,0:T(8,128)(2,1)S(1)}, bf16[128,2048]{1,0:T(8,128)(2,1)}, u32[]{:S(2)}) copy-start(bf16[128,2048]{1,0:T(8,128)(2,1)} %get-tuple-element.19) | copy-start | bytes 1572868
  144.7 1.9 %copy-start.4 = (f32[256,512]{1,0:T(8,128)S(1)}, f32[256,512]{1,0:T(8,128)}, u32[]{:S(2)}) copy-start(f32[256,512]{1,0:T(8,128)} %get-tuple-element.36) | copy-start | bytes 1572868
  144.7 2.7 %copy-start.3 = (f32[256,512]{1,0:T(8,128)S(1)}, f32[256,512]{1,0:T(8,128)}, u32[]{:S(2)}) copy-start(f32[256,512]{1,0:T(8,128)} %get-tuple-element.37) | copy-start | bytes 1572868
